TPU v7x, 32 devices: a whole 2x2x4 slice. The times are simulated.
32 devices in a mesh: comp: 4 (over x, core), mom: 8 (over z, y).
Axes of the slice: x: 2, y: 2, z: 4, core: 2. Of those that a mesh axis runs over, the one named last changes fastest.
Arguments:
- green_guess: float32 [4, 512, 192, 384], P('comp', 'mom'), may hold values from -3 to 3
- green_free: float32 [4, 512, 192, 384], P('comp', 'mom'), may hold values from -3 to 3
- retarded: float32 [512, 192, 384], P('mom'), may hold values from -0.3125 to 0.3125
- momentum_order: int32 [512], replicated, may hold values from 0 to 511, each once
Outputs:
- green_final: float32 [4, 512, 192, 384], P('comp', 'mom')
- self_energy: float32 [4, 512, 192, 384], P('comp', 'mom')
Inputs may be any that keep to these rules, and one draw needn't show every extreme that they name: `momentum_order`: a permutation of the lattice momenta 0 to 511.
All inputs are finite; a program needn't handle non-finite values.
Results may differ from a plain program's by a relative error of at most 0.00013.
Values sent between devices are 32-bit elements; how exact they have to be, the bound alone decides.
A program may use at most 192 MiB of HBM per device.

v0:
```python
import math

import jax
import jax.numpy as jnp
from jax import lax
from jax.sharding import PartitionSpec as P

K = 512
L1 = 16


highest = lax.Precision.HIGHEST


def partner(x, axis, bit):
    return lax.ppermute(x, axis, [(i, i ^ 1 << bit) for i in range(lax.axis_size(axis))])


def phase_tables(momentum_order, count, first_len):
    second_len = count // first_len
    site_ids = jnp.arange(count, dtype=jnp.int32)
    site_one = site_ids // second_len
    site_two = site_ids % second_len
    mom_one = momentum_order // second_len
    mom_two = momentum_order % second_len
    phases = (
        site_one[:, None] * mom_one[None, :] * second_len
        + site_two[:, None] * mom_two[None, :] * first_len
    ) % count
    angles = phases.astype(jnp.float32) * (2.0 * math.pi / count)
    norm_factor = 1.0 / math.sqrt(count)
    return (jnp.cos(angles) * norm_factor, jnp.sin(angles) * norm_factor)


def forward_transform(values, cosine, sine_table, half_width):
    full_shape = values.shape
    flattened = values.reshape(full_shape[0], -1)
    with_cos = jnp.dot(
        cosine, flattened, precision=highest, preferred_element_type=jnp.float32
    ).reshape(full_shape)
    with_sin = jnp.dot(
        sine_table, flattened, precision=highest, preferred_element_type=jnp.float32
    ).reshape(full_shape)
    real_part = with_cos[..., :half_width] - with_sin[..., half_width:]
    imag_part = with_cos[..., half_width:] + with_sin[..., :half_width]
    return jnp.concatenate([real_part, imag_part], axis=-1)


def inverse_transform(values, cos_back, sin_back, half_width):
    full_shape = values.shape
    flattened = values.reshape(full_shape[0], -1)
    with_cos = jnp.dot(
        cos_back, flattened, precision=highest, preferred_element_type=jnp.float32
    ).reshape(full_shape)
    with_sin = jnp.dot(
        sin_back, flattened, precision=highest, preferred_element_type=jnp.float32
    ).reshape(full_shape)
    real_part = with_cos[..., :half_width] + with_sin[..., half_width:]
    imag_part = with_cos[..., half_width:] - with_sin[..., :half_width]
    return jnp.concatenate([real_part, imag_part], axis=-1)


def triple(own_part, second, conj_factor, half_width):
    prod_real = (
        own_part[..., :half_width] * second[..., :half_width]
        - own_part[..., half_width:] * second[..., half_width:]
    )
    prod_imag = (
        own_part[..., :half_width] * second[..., half_width:]
        + own_part[..., half_width:] * second[..., :half_width]
    )
    conj_real = conj_factor[..., :half_width]
    conj_imag = conj_factor[..., half_width:]
    real_part = prod_real * conj_real + prod_imag * conj_imag
    imag_part = prod_imag * conj_real - prod_real * conj_imag
    return -jnp.concatenate([real_part, imag_part], axis=-1)


def dyson(sigma_mom, retarded, free_part, half_width):
    ret_real = retarded[..., :half_width]
    ret_imag = retarded[..., half_width:]
    swapped = jnp.concatenate([-sigma_mom[..., half_width:], sigma_mom[..., :half_width]], axis=-1)
    left_prod = jnp.einsum(
        "kij,kjx->kix", ret_real, sigma_mom, precision=highest, preferred_element_type=jnp.float32
    )
    left_prod = left_prod + jnp.einsum(
        "kij,kjx->kix", ret_imag, swapped, precision=highest, preferred_element_type=jnp.float32
    )
    turned = jnp.concatenate([left_prod[..., half_width:], -left_prod[..., :half_width]], axis=-1)
    real_part = jnp.einsum(
        "kim,kjm->kij", left_prod, retarded, precision=highest, preferred_element_type=jnp.float32
    )
    imag_part = jnp.einsum(
        "kim,kjm->kij", turned, retarded, precision=highest, preferred_element_type=jnp.float32
    )
    return free_part + jnp.concatenate([real_part, imag_part], axis=-1)


def on_device(green_guess, green_free, retarded, momentum_order):
    mom_count = lax.axis_size("mom")
    half_width = green_guess.shape[-1] // 2
    k_local = green_guess.shape[1]
    tile_rows = half_width // mom_count
    cosine, sine_table = phase_tables(momentum_order, K, L1)
    cos_back = cosine.T
    sin_back = sine_table.T
    free_local = green_free[0]
    current = green_guess[0]
    tiled = current.reshape(k_local, mom_count, tile_rows, 2 * half_width)
    in_sites = forward_transform(
        lax.all_to_all(tiled, "mom", split_axis=1, concat_axis=0, tiled=True),
        cosine,
        sine_table,
        half_width,
    )
    spin_other = partner(in_sites, "comp", 1)
    cross_other = partner(spin_other, "comp", 0)
    sigma_sites = triple(in_sites, spin_other, cross_other, half_width)
    momentum_tile = inverse_transform(sigma_sites, cos_back, sin_back, half_width)
    restored = lax.all_to_all(momentum_tile, "mom", split_axis=0, concat_axis=1, tiled=True)
    sigma_mom = restored.reshape(k_local, mom_count * tile_rows, 2 * half_width)
    current = dyson(sigma_mom, retarded, free_local, half_width)
    return (current[None], sigma_mom[None])


def solution(mesh):
    return jax.shard_map(
        on_device,
        mesh=mesh,
        in_specs=(
            P("comp", "mom", None, None),
            P("comp", "mom", None, None),
            P("mom", None, None),
            P(),
        ),
        out_specs=(P("comp", "mom", None, None), P("comp", "mom", None, None)),
        check_vma=False,
    )
```

profile of v0, /device:TPU:0, one launch (start us, length us, event | category | flops | bytes accessed | tf_op | source)
XLA Modules:
  0.0 1808.6 jit_solution(11912606751356150233)
XLA Ops:
  0.6 14.4 copy.18
  15.0 7.4 all-to-all-start
  22.5 408.2 %all-to-all-done = f32[64,8,24,384]{3,2,0,1:T(8,128)} async-done(((f32[64,8,24,384]{3,2,0,1:T(8,128)}), f32[64,8,24,384]{3,2,0,1:T(8,128)}, u32[]{:S(2)}, u32[]{:S(2)}) %all-to-all-start) | async-done | bytes 18874400 | tf_op jit(solution)/shard_map/all_to_all | solution.py:111
  430.7 17.8 copy.23
  448.5 18.6 %copy.19 = f32[9216,512]{1,0:T(8,128)} copy(f32[9216,512]{0,1:T(8,128)} %bitcast.62) | data formatting | bytes 37748736 | tf_op jit(solution)/shard_map/dot_general | solution.py:38
  467.1 51.4 %convolution_bitcast_fusion = f32[512,1,24,384]{0,3,2,1:T(8,128)} fusion(f32[24,384,512]{2,1,0:T(8,128)} %bitcast.60, s32[512]{0:T(512)S(1)} %get-tuple-element.14, s32[512]{0:T(512)S(1)} %get-tuple-element.15, s32[512]{0:T(512)S(1)} %get-tuple-element.13, s32[512]{0:T(512)S(1)} %add_select_fusion.3), kind=kOutput, calls=%fused_computation.30 | convolution fusion | flops 28996009984 | bytes 37756928 | tf_op jit(solution)/shard_map/dot_general | solution.py:41
  518.6 46.6 %convolution_bitcast_fusion.1 = f32[512,1,24,384]{0,3,2,1:T(8,128)} fusion(f32[24,384,512]{2,1,0:T(8,128)S(1)} %bitcast.61, s32[512]{0:T(512)S(1)} %get-tuple-element.14, s32[512]{0:T(512)S(1)} %get-tuple-element.15, s32[512]{0:T(512)S(1)} %get-tuple-element.13, s32[512]{0:T(512)S(1)} %add_select_fusion.3), kind=kOutput, calls=%fused_computation.31 | convolution fusion | flops 28996009984 | bytes 37756928 | tf_op jit(solution)/shard_map/dot_general | solution.py:38
  565.1 13.6 slice_subtract_fusion.1
  578.8 8.0 pad_maximum_fusion
  588.1 3.3 copy-done.3
  591.3 1.4 collective-permute-start
  592.7 404.8 %collective-permute-done = f32[512,1,24,384]{0,3,2,1:T(8,128)S(1)} collective-permute-done((f32[512,1,24,384]{0,3,2,1:T(8,128)}, f32[512,1,24,384]{0,3,2,1:T(8,128)S(1)}, u32[]{:S(2)}, u32[]{:S(2)}) %collective-permute-start) | collective-permute-done | bytes 18874400 | tf_op jit(solution)/shard_map/ppermute | solution.py:16
  997.5 6.8 copy-done.4
  1004.4 28.3 %collective-permute-done.1 = f32[512,1,24,384]{0,3,2,1:T(8,128)} collective-permute-done((f32[512,1,24,384]{0,3,2,1:T(8,128)S(1)}, f32[512,1,24,384]{0,3,2,1:T(8,128)}, u32[]{:S(2)}, u32[]{:S(2)}) %collective-permute-start.1) | collective-permute-done | bytes 18874400 | tf_op jit(solution)/shard_map/ppermute | solution.py:16
  1032.6 31.0 %multiply_add_fusion = (f32[512,1,24,192]{0,3,2,1:T(8,128)}, f32[512,1,24,192]{0,3,2,1:T(8,128)}, f32[512,1,24,192]{0,3,2,1:T(8,128)}) fusion(f32[512,1,24,384]{0,3,2,1:T(8,128)} %collective-permute-done.1, f32[512,1,24,192]{0,3,2,1:T(8,128)} %copy-done.3, f32[512,1,24,384]{0,3,2,1:T(8,128)} %copy-done.4, f32[512,1,24,192]{0,3,2,1:T(8,128)} %copy-done.2), kind=kLoop, calls=%fused_computation.25 | loop fusion | flops 21233664 | bytes 84934656 | tf_op jit(solution)/shard_map/add | solution.py:74
  1063.7 17.8 multiply_subtract_fusion
  1081.5 46.1 %fusion.19 = f32[512,1,24,384]{0,3,2,1:T(8,128)} fusion(f32[512,1,24,192]{0,3,2,1:T(8,128)} %multiply_subtract_fusion, f32[512,1,24,192]{0,3,2,1:T(8,128)S(1)} %copy-done.5, s32[512]{0:T(512)S(1)} %get-tuple-element.14, s32[512]{0:T(512)S(1)} %get-tuple-element.15, s32[512]{0:T(512)S(1)} %get-tuple-element.13, s32[512]{0:T(512)S(1)} %add_select_fusion.3), kind=kOutput, calls=%fused_computation.29 | convolution fusion | flops 29005447168 | bytes 37756928 | tf_op jit(solution)/shard_map/dot_general | solution.py:55
  1127.6 46.4 %fusion.16 = f32[512,1,24,384]{0,3,2,1:T(8,128)} fusion(f32[512,1,24,192]{0,3,2,1:T(8,128)} %multiply_subtract_fusion, f32[512,1,24,192]{0,3,2,1:T(8,128)S(1)} %copy-done.5, s32[512]{0:T(512)S(1)} %get-tuple-element.14, s32[512]{0:T(512)S(1)} %get-tuple-element.15, s32[512]{0:T(512)S(1)} %get-tuple-element.13, s32[512]{0:T(512)S(1)} %add_select_fusion.3), kind=kOutput, calls=%fused_computation.28 | convolution fusion | flops 29005447168 | bytes 37756928 | tf_op jit(solution)/shard_map/dot_general | solution.py:52
  1173.9 13.6 slice_add_fusion
  1187.6 7.1 pad_maximum_fusion.1
  1194.7 18.9 %copy.20 = f32[512,1,24,384]{3,2,1,0:T(8,128)} copy(f32[512,1,24,384]{0,3,2,1:T(8,128)} %pad_maximum_fusion.1) | data formatting | bytes 37748736 | tf_op jit(solution)/shard_map/concatenate | solution.py:60
  1213.6 412.6 %all_to_all.30 = f32[512,1,24,384]{3,2,1,0:T(8,128)S(1)} all-to-all(f32[512,1,24,384]{3,2,1,0:T(8,128)} %copy.20), channel_id=1, replica_groups=mesh['comp'=4,'mom'=8] {'mom'}, dimensions={0} | all-to-all | bytes 37748736 | tf_op jit(solution)/shard_map/all_to_all | solution.py:120
  1626.2 2.5 copy.21
  1628.7 6.8 copy-done
  1635.5 10.0 slice_negate_fusion.1
  1645.5 27.5 %fusion.14 = f32[64,384,192]{1,2,0:T(8,128)} fusion(f32[64,192,384]{2,1,0:T(8,128)} %bitcast.58, f32[64,192,384]{2,1,0:T(8,128)} %param.6), kind=kOutput, calls=%fused_computation.18 | convolution fusion | flops 10871635968 | bytes 50331648 | tf_op jit(solution)/shard_map/kij,kjx->kix/dot_general | solution.py:83
  1673.0 31.5 %fusion.1 = f32[64,384,192]{1,2,0:T(8,128)} fusion(f32[64,192,192]{2,1,0:T(8,128)} %get-tuple-element.12, f32[64,192,192]{2,1,0:T(8,128)} %get-tuple-element.11, f32[64,192,384]{2,1,0:T(8,128)} %param.6), kind=kOutput, calls=%fused_computation.4 | convolution fusion | flops 10876354560 | bytes 56623104 | tf_op jit(solution)/shard_map/kij,kjx->kix/dot_general | solution.py:86
  1704.5 30.1 %fusion.24 = f32[1,64,192,192]{3,2,1,0:T(8,128)} fusion(f32[64,192,384]{2,1,0:T(8,128)} %param.6, f32[64,384,192]{1,2,0:T(8,128)} %fusion.14, f32[64,384,192]{1,2,0:T(8,128)} %fusion.1), kind=kOutput, calls=%fused_computation.35 | convolution fusion | flops 10876354560 | bytes 66060288 | tf_op jit(solution)/shard_map/kim,kjm->kij/dot_general | solution.py:90
  1734.5 12.5 add_bitcast_fusion
  1747.0 10.1 fusion.85
  1757.1 29.2 %fusion.27 = f32[1,64,192,192]{3,2,1,0:T(8,128)} fusion(f32[64,192,384]{2,1,0:T(8,128)} %param.6, f32[64,192,192]{2,1,0:T(8,128)} %get-tuple-element.10, f32[64,192,192]{2,1,0:T(8,128)} %get-tuple-element.9), kind=kOutput, calls=%fused_computation.36 | convolution fusion | flops 10876354560 | bytes 47185920 | tf_op jit(solution)/shard_map/kim,kjm->kij/dot_general | solution.py:93
  1786.3 22.1 %maximum_add_fusion = f32[1,64,192,384]{3,2,1,0:T(8,128)} fusion(f32[1,64,192,384]{3,2,1,0:T(8,128)} %param.5, f32[1,64,192,192]{3,2,1,0:T(8,128)} %fusion.27, f32[1,64,192,192]{3,2,1,0:T(8,128)} %fusion.24), kind=kLoop, calls=%fused_computation.12 | loop fusion | flops 9437184 | bytes 56623104 | tf_op jit(solution)/shard_map/add | solution.py:96
  (14 shorter events, 1.3 us)
Async XLA Ops:
  15.0 7.5 copy-start.6
  15.0 415.7 %all-to-all-start = ((f32[64,8,24,384]{3,2,0,1:T(8,128)}), f32[64,8,24,384]{3,2,0,1:T(8,128)}, u32[]{:S(2)}, u32[]{:S(2)}) async-start(f32[64,8,24,384]{3,2,0,1:T(8,128)} %copy.18), calls=%async_computation | async-start | bytes 37748736 | tf_op jit(solution)/shard_map/all_to_all | solution.py:111
  467.1 51.4 %copy-start.1 = (f32[9216,512]{1,0:T(8,128)S(1)}, f32[9216,512]{1,0:T(8,128)}, u32[]{:S(2)}) copy-start(f32[9216,512]{1,0:T(8,128)} %copy.19) | copy-start | bytes 56623108
  578.8 9.3 copy-start.2
  578.8 12.5 copy-start.3
  591.3 406.2 %collective-permute-start = (f32[512,1,24,384]{0,3,2,1:T(8,128)}, f32[512,1,24,384]{0,3,2,1:T(8,128)S(1)}, u32[]{:S(2)}, u32[]{:S(2)}) collective-permute-start(f32[512,1,24,384]{0,3,2,1:T(8,128)} %pad_maximum_fusion), channel_id=1, source_target_pairs={{0,16},{8,24},{16,0},{24,8},{1,17},{9,25},{17,1},{25,9},{2,18},{10... | collective-permute-start | bytes 56623112 | tf_op jit(solution)/shard_map/ppermute | solution.py:16
  997.5 6.9 copy-start.4
  1004.4 28.3 %collective-permute-start.1 = (f32[512,1,24,384]{0,3,2,1:T(8,128)S(1)}, f32[512,1,24,384]{0,3,2,1:T(8,128)}, u32[]{:S(2)}, u32[]{:S(2)}) collective-permute-start(f32[512,1,24,384]{0,3,2,1:T(8,128)S(1)} %collective-permute-done), channel_id=1, source_target_pairs={{0,8},{8,0},{16,24},{24,16},{1,9},{9,1},{17,25},{25,17},{2,10},{10... | collective-permute-start | bytes 56623112 | tf_op jit(solution)/shard_map/ppermute | solution.py:16
  1063.7 17.8 copy-start.5
  1628.6 6.9 copy-start
where the time goes:
time: 1810 us
  waiting for transfers between devices  841 us (46%)
  blocking collectives  413 us (23%)
  matrix products  309 us (17%)
  other arithmetic  146 us (8%)
  local copies, waits for them, and re-layouts  90.3 us (5%)
    ppermute x2, waiting for transfers between devices, partner(): lax.ppermute(x, axis, [(i, i ^ 1 << bit) for i in range(lax.axis_size(axi...  433 us
    all_to_all x1, blocking collectives, on_device(): lax.all_to_all(momentum_tile, 'mom', split_axis=0, concat_axis=1, tiled=T...  413 us
    all_to_all x1, waiting for transfers between devices, on_device(): lax.all_to_all(tiled, 'mom', split_axis=1, concat_axis=0, tiled=True)  408 us
    dot_general x1, matrix products, forward_transform(): jnp.dot(sine_table, flattened, precision=highest, preferred_element_type=...  51.4 us
    dot_general x1, matrix products, forward_transform(): jnp.dot(cosine, flattened, precision=highest, preferred_element_type=jnp....  46.6 us
    dot_general x1, matrix products, inverse_transform(): jnp.dot(cos_back, flattened, precision=highest, preferred_element_type=jn...  46.4 us
    dot_general x1, matrix products, inverse_transform(): jnp.dot(sin_back, flattened, precision=highest, preferred_element_type=jn...  46.1 us
  transfers between devices with their start and end apart: 3, of which 3 were waited for; matrix products, arithmetic and copies ran while one was open for 0% of the time, Pallas kernels for 0%

commit v1 on v0

--- a/solution.py
+++ b/solution.py
@@ -9,7 +9,7 @@
 L1 = 16
 
 
-highest = lax.Precision.HIGHEST
+highest = lax.Precision.HIGH
 
 
 def partner(x, axis, bit):
@@ -96,31 +96,47 @@
     return free_part + jnp.concatenate([real_part, imag_part], axis=-1)
 
 
+CHUNKS = 3
+GROUPS = 4
+
+
+def exchange(send, axis):
+    size = lax.axis_size(axis)
+    return [send[0]] + [
+        lax.ppermute(send[s], axis, [(i, i ^ s) for i in range(size)]) for s in range(1, size)
+    ]
+
+
 def on_device(green_guess, green_free, retarded, momentum_order):
     mom_count = lax.axis_size("mom")
-    half_width = green_guess.shape[-1] // 2
+    me = lax.axis_index("mom")
+    width = green_guess.shape[-1]
+    half_width = width // 2
     k_local = green_guess.shape[1]
     tile_rows = half_width // mom_count
+    rows = tile_rows // CHUNKS
+    group = k_local // GROUPS
     cosine, sine_table = phase_tables(momentum_order, K, L1)
     cos_back = cosine.T
     sin_back = sine_table.T
     free_local = green_free[0]
     current = green_guess[0]
-    tiled = current.reshape(k_local, mom_count, tile_rows, 2 * half_width)
-    in_sites = forward_transform(
-        lax.all_to_all(tiled, "mom", split_axis=1, concat_axis=0, tiled=True),
-        cosine,
-        sine_table,
-        half_width,
-    )
-    spin_other = partner(in_sites, "comp", 1)
-    cross_other = partner(spin_other, "comp", 0)
-    sigma_sites = triple(in_sites, spin_other, cross_other, half_width)
-    momentum_tile = inverse_transform(sigma_sites, cos_back, sin_back, half_width)
-    restored = lax.all_to_all(momentum_tile, "mom", split_axis=0, concat_axis=1, tiled=True)
-    sigma_mom = restored.reshape(k_local, mom_count * tile_rows, 2 * half_width)
-    current = dyson(sigma_mom, retarded, free_local, half_width)
-    return (current[None], sigma_mom[None])
+
+    tiled = current.reshape(k_local, mom_count, CHUNKS, rows, width)
+    arrived = [
+        lax.all_to_all(tiled[:, :, c], "mom", split_axis=1, concat_axis=0, tiled=True)
+        for c in range(CHUNKS)
+    ]
+    pieces = []
+    for c in range(CHUNKS):
+        in_sites = forward_transform(arrived[c][:, 0], cosine, sine_table, half_width)
+        spin_other = partner(in_sites, "comp", 1)
+        cross_other = partner(spin_other, "comp", 0)
+        sigma_sites = triple(in_sites, spin_other, cross_other, half_width)
+        tile = inverse_transform(sigma_sites, cos_back, sin_back, half_width)
+        pieces.append(lax.all_to_all(tile.reshape(mom_count, k_local, 1, rows, width), "mom", split_axis=0, concat_axis=2, tiled=True))
+    sigma = jnp.stack(pieces, axis=3).reshape(k_local, half_width, width)
+    return (dyson(sigma, retarded, free_local, half_width)[None], sigma[None])
 
 
 def solution(mesh):

time: 1810 us -> 1100 us (0.61)
  blocking collectives: 413 us -> 0 us
  waiting for transfers between devices: 841 us -> 570 us
  matrix products: 309 us -> 232 us
  starting transfers between devices: 8.87 us -> 38.1 us
  local copies, waits for them, and re-layouts: 90.3 us -> 115 us
    all_to_all x1 -> x0, blocking collectives: 413 us -> none  [on_device(): lax.all_to_all(momentum_tile, 'mom', split_axis=0, concat_axis=1, tiled=T...]
    ppermute x2 -> x6, waiting for transfers between devices: 433 us -> 220 us  [partner(): lax.ppermute(x, axis, [(i, i ^ 1 << bit) for i in range(lax.axis_size(axi...]
    all_to_all x1 -> x6, waiting for transfers between devices: 408 us -> 351 us  [the longest x3 225 us: on_device(): lax.all_to_all(tiled[:, :, c], 'mom', split_axis=1, concat_axis=0, tiled=...]
    all_to_all x1 -> x6, starting transfers between devices: 7.44 us -> 33.6 us  [the longest x3 16.9 us: on_device(): lax.all_to_all(tiled[:, :, c], 'mom', split_axis=1, concat_axis=0, tiled=...]
    dot_general x1 -> x3, matrix products: 46.4 us -> 27.8 us  [inverse_transform(): jnp.dot(cos_back, flattened, precision=highest, preferred_element_type=jn...]
    dot_general x1 -> x3, matrix products: 51.4 us -> 36.3 us  [forward_transform(): jnp.dot(sine_table, flattened, precision=highest, preferred_element_type=...]
    dot_general x1 -> x3, matrix products: 46.6 us -> 33.7 us  [forward_transform(): jnp.dot(cosine, flattened, precision=highest, preferred_element_type=jnp....]
    dot_general x1 -> x3, matrix products: 46.1 us -> 34.5 us  [inverse_transform(): jnp.dot(sin_back, flattened, precision=highest, preferred_element_type=jn...]
  transfers between devices with their start and end apart: 3 -> 12, of which waited for: 3 -> 8; matrix products, arithmetic and copies ran while one was open for 0% -> 26% of each run, Pallas kernels for 0% -> 0%
where the time goes in v1:
time: 1100 us; the launch traced here: 1090 us
  waiting for transfers between devices  570 us (52%)
  matrix products  232 us (21%)
  other arithmetic  128 us (12%)
  local copies, waits for them, and re-layouts  115 us (10%)
  starting transfers between devices  38.1 us (3%)
    all_to_all x3, waiting for transfers between devices, on_device(): lax.all_to_all(tiled[:, :, c], 'mom', split_axis=1, concat_axis=0, tiled=...  225 us
    ppermute x6, waiting for transfers between devices, partner(): lax.ppermute(x, axis, [(i, i ^ 1 << bit) for i in range(lax.axis_size(axi...  220 us
    all_to_all x3, waiting for transfers between devices, on_device(): lax.all_to_all(tile.reshape(mom_count, k_local, 1, rows, width), 'mom', s...  126 us
    unnamed x44, local copies, waits for them, and re-layouts  44 us
    dot_general x3, matrix products, forward_transform(): jnp.dot(sine_table, flattened, precision=highest, preferred_element_type=...  36.3 us
    dot_general x3, matrix products, inverse_transform(): jnp.dot(sin_back, flattened, precision=highest, preferred_element_type=jn...  34.5 us
    dot_general x3, matrix products, forward_transform(): jnp.dot(cosine, flattened, precision=highest, preferred_element_type=jnp....  33.7 us
    dot_general x3, matrix products, inverse_transform(): jnp.dot(cos_back, flattened, precision=highest, preferred_element_type=jn...  27.8 us
  transfers between devices with their start and end apart: 12, of which 8 were waited for; matrix products, arithmetic and copies ran while one was open for 26% of the time, Pallas kernels for 0%

profile of v1, /device:TPU:0, one launch (start us, length us, event | category | flops | bytes accessed | tf_op | source)
XLA Modules:
  0.0 1086.0 jit_solution(13214193050168592810)
XLA Ops:
  0.6 12.0 %fusion.156 = (f32[64,8,1,8,384]{4,3,2,1,0:T(8,128)S(1)}, f32[64,8,1,8,384]{4,3,2,1,0:T(8,128)}, f32[64,8,1,8,384]{4,3,2,1,0:T(8,128)}) fusion(f32[64,8,3,8,384]{4,3,2,1,0:T(8,128)} %bitcast.154), kind=kLoop, calls=%fused_computation.206 | loop fusion | bytes 37748736 | tf_op jit(solution)/shard_map/slice | solution.py:127
  15.8 7.3 all-to-all-start
  28.9 132.4 %all-to-all-done = f32[64,8,8,384]{3,2,0,1:T(8,128)} async-done(((f32[64,8,8,384]{3,2,0,1:T(8,128)}), f32[64,8,8,384]{3,2,0,1:T(8,128)}, u32[]{:S(2)}, u32[]{:S(2)}) %all-to-all-start) | async-done | bytes 6291488 | tf_op jit(solution)/shard_map/all_to_all | solution.py:127
  166.2 6.9 copy.50
  179.6 12.2 %fusion.44 = f32[512,8,384]{0,2,1:T(8,128)S(1)} fusion(f32[8,384,512]{2,1,0:T(8,128)} %bitcast.134, s32[512]{0:T(512)S(1)} %get-tuple-element.31, s32[512]{0:T(512)S(1)} %get-tuple-element.32, s32[512]{0:T(512)S(1)} %get-tuple-element.30, s32[512]{0:T(512)S(1)} %add_select_fusion.3), kind=kOutput, calls=%fused_computation.81 | convolution fusion | flops 4836818944 | bytes 12591104 | tf_op jit(solution)/shard_map/dot_general | solution.py:41
  191.9 11.6 %fusion.53 = f32[512,8,384]{0,2,1:T(8,128)} fusion(f32[8,384,512]{2,1,0:T(8,128)S(1)} %bitcast.135, s32[512]{0:T(512)S(1)} %get-tuple-element.31, s32[512]{0:T(512)S(1)} %get-tuple-element.32, s32[512]{0:T(512)S(1)} %get-tuple-element.30, s32[512]{0:T(512)S(1)} %add_select_fusion.3), kind=kOutput, calls=%fused_computation.90 | convolution fusion | flops 4836818944 | bytes 12591104 | tf_op jit(solution)/shard_map/dot_general | solution.py:38
  217.1 86.4 %all-to-all-done.2 = f32[64,8,8,384]{3,2,0,1:T(8,128)} async-done(((f32[64,8,8,384]{3,2,0,1:T(8,128)}), f32[64,8,8,384]{3,2,0,1:T(8,128)}, u32[]{:S(2)}, u32[]{:S(2)}) %all-to-all-start.2) | async-done | bytes 6291488 | tf_op jit(solution)/shard_map/all_to_all | solution.py:127
  308.2 40.7 %collective-permute-done = f32[512,8,384]{0,2,1:T(8,128)} collective-permute-done((f32[512,8,384]{0,2,1:T(8,128)}, f32[512,8,384]{0,2,1:T(8,128)}, u32[]{:S(2)}, u32[]{:S(2)}) %collective-permute-start) | collective-permute-done | bytes 6291488 | tf_op jit(solution)/shard_map/ppermute | solution.py:16
  349.0 6.9 copy.51
  355.8 7.0 copy.38
  362.9 12.2 %fusion.41 = f32[512,8,384]{0,2,1:T(8,128)S(1)} fusion(f32[8,384,512]{2,1,0:T(8,128)} %bitcast.136, s32[512]{0:T(512)S(1)} %get-tuple-element.31, s32[512]{0:T(512)S(1)} %get-tuple-element.32, s32[512]{0:T(512)S(1)} %get-tuple-element.30, s32[512]{0:T(512)S(1)} %add_select_fusion.3), kind=kOutput, calls=%fused_computation.78 | convolution fusion | flops 4836818944 | bytes 12591104 | tf_op jit(solution)/shard_map/dot_general | solution.py:41
  375.1 9.9 fusion.50
  403.4 9.3 fusion.26
  412.7 12.2 %fusion.24 = f32[512,8,384]{0,2,1:T(8,128)} fusion(f32[512,8,192]{0,2,1:T(8,128)S(1)} %multiply_subtract_fusion.4, f32[512,8,192]{0,2,1:T(8,128)S(1)} %get-tuple-element.2, s32[512]{0:T(512)S(1)} %get-tuple-element.31, s32[512]{0:T(512)S(1)} %get-tuple-element.32, s32[512]{0:T(512)S(1)} %get-tuple-element.30, s32[512]{0:T(512)S(1)} %add_select_fusion.3), kind=kOutput, calls=%fused_computation.40 | convolution fusion | flops 4839964672 | bytes 12591104 | tf_op jit(solution)/shard_map/dot_general | solution.py:55
  450.4 79.2 %collective-permute-done.2 = f32[512,8,384]{0,2,1:T(8,128)} collective-permute-done((f32[512,8,384]{0,2,1:T(8,128)}, f32[512,8,384]{0,2,1:T(8,128)}, u32[]{:S(2)}, u32[]{:S(2)}) %collective-permute-start.2) | collective-permute-done | bytes 6291488 | tf_op jit(solution)/shard_map/ppermute | solution.py:16
  543.0 12.2 %fusion.47 = f32[512,8,384]{0,2,1:T(8,128)S(1)} fusion(f32[8,384,512]{2,1,0:T(8,128)} %bitcast.138, s32[512]{0:T(512)S(1)} %get-tuple-element.31, s32[512]{0:T(512)S(1)} %get-tuple-element.32, s32[512]{0:T(512)S(1)} %get-tuple-element.30, s32[512]{0:T(512)S(1)} %add_select_fusion.3), kind=kOutput, calls=%fused_computation.84 | convolution fusion | flops 4836818944 | bytes 12591104 | tf_op jit(solution)/shard_map/dot_general | solution.py:38
  555.2 11.9 %fusion.38 = f32[512,8,384]{0,2,1:T(8,128)} fusion(f32[8,384,512]{2,1,0:T(8,128)S(1)} %bitcast.139, s32[512]{0:T(512)S(1)} %get-tuple-element.31, s32[512]{0:T(512)S(1)} %get-tuple-element.32, s32[512]{0:T(512)S(1)} %get-tuple-element.30, s32[512]{0:T(512)S(1)} %add_select_fusion.3), kind=kOutput, calls=%fused_computation.75 | convolution fusion | flops 4836818944 | bytes 12591104 | tf_op jit(solution)/shard_map/dot_general | solution.py:41
  588.9 9.3 fusion.22
  598.2 9.6 fusion.20
  625.6 89.4 %collective-permute-done.4 = f32[512,8,384]{0,2,1:T(8,128)} collective-permute-done((f32[512,8,384]{0,2,1:T(8,128)}, f32[512,8,384]{0,2,1:T(8,128)}, u32[]{:S(2)}, u32[]{:S(2)}) %collective-permute-start.4) | collective-permute-done | bytes 6291488 | tf_op jit(solution)/shard_map/ppermute | solution.py:16
  715.0 10.4 collective-permute-done.5
  734.0 9.3 fusion.18
  743.3 12.6 %fusion.16 = f32[512,8,384]{0,2,1:T(8,128)S(1)} fusion(f32[512,8,192]{0,2,1:T(8,128)} %copy-done.15, f32[512,8,192]{0,2,1:T(8,128)} %copy-done.14, s32[512]{0:T(512)S(1)} %get-tuple-element.31, s32[512]{0:T(512)S(1)} %get-tuple-element.32, s32[512]{0:T(512)S(1)} %get-tuple-element.30, s32[512]{0:T(512)S(1)} %add_select_fusion.3), kind=kOutput, calls=%fused_computation.36 | convolution fusion | flops 4839964672 | bytes 12591104 | tf_op jit(solution)/shard_map/dot_general | solution.py:55
  786.3 125.8 %all-to-all-done.5 = f32[8,64,1,8,384]{4,3,1,2,0:T(8,128)} async-done(((f32[8,64,1,8,384]{4,3,1,2,0:T(8,128)}), f32[8,64,1,8,384]{4,3,1,2,0:T(8,128)}, u32[]{:S(2)}, u32[]{:S(2)}) %all-to-all-start.5) | async-done | bytes 6291488 | tf_op jit(solution)/shard_map/all_to_all | solution.py:137
  931.0 9.9 slice_negate_fusion.1
  940.9 25.7 %fusion.9 = f32[64,384,192]{1,2,0:T(8,128)} fusion(f32[64,192,384]{2,1,0:T(8,128)} %bitcast.132, f32[64,192,384]{2,1,0:T(8,128)} %param.6), kind=kOutput, calls=%fused_computation.13 | convolution fusion | flops 5435817984 | bytes 50331648 | tf_op jit(solution)/shard_map/kij,kjx->kix/dot_general | solution.py:83
  966.6 26.0 %fusion = f32[64,384,192]{1,2,0:T(8,128)} fusion(f32[64,192,192]{2,1,0:T(8,128)} %get-tuple-element.14, f32[64,192,192]{2,1,0:T(8,128)} %get-tuple-element.13, f32[64,192,384]{2,1,0:T(8,128)} %param.6), kind=kOutput, calls=%fused_computation.1 | convolution fusion | flops 5440536576 | bytes 56623104 | tf_op jit(solution)/shard_map/kij,kjx->kix/dot_general | solution.py:86
  992.6 24.4 %fusion.28 = f32[1,64,192,192]{3,2,1,0:T(8,128)} fusion(f32[64,192,384]{2,1,0:T(8,128)} %param.6, f32[64,384,192]{1,2,0:T(8,128)} %fusion.9, f32[64,384,192]{1,2,0:T(8,128)} %fusion), kind=kOutput, calls=%fused_computation.42 | convolution fusion | flops 5440536576 | bytes 66060288 | tf_op jit(solution)/shard_map/kim,kjm->kij/dot_general | solution.py:90
  1016.9 12.5 %add_bitcast_fusion = f32[64,192,384]{2,1,0:T(8,128)S(1)} fusion(f32[64,384,192]{1,2,0:T(8,128)} %fusion.9, f32[64,384,192]{1,2,0:T(8,128)} %fusion), kind=kLoop, calls=%fused_computation.15 | loop fusion | flops 4718592 | bytes 56623104 | tf_op jit(solution)/shard_map/add | solution.py:86
  1029.4 10.0 fusion.155
  1039.5 24.0 %fusion.31 = f32[1,64,192,192]{3,2,1,0:T(8,128)} fusion(f32[64,192,384]{2,1,0:T(8,128)} %param.6, f32[64,192,192]{2,1,0:T(8,128)} %get-tuple-element.12, f32[64,192,192]{2,1,0:T(8,128)} %get-tuple-element.11), kind=kOutput, calls=%fused_computation.43 | convolution fusion | flops 5440536576 | bytes 47185920 | tf_op jit(solution)/shard_map/kim,kjm->kij/dot_general | solution.py:93
  1063.4 22.1 %maximum_add_fusion = f32[1,64,192,384]{3,2,1,0:T(8,128)} fusion(f32[1,64,192,384]{3,2,1,0:T(8,128)} %param.5, f32[1,64,192,192]{3,2,1,0:T(8,128)} %fusion.31, f32[1,64,192,192]{3,2,1,0:T(8,128)} %fusion.28), kind=kLoop, calls=%fused_computation.9 | loop fusion | flops 9437184 | bytes 56623104 | tf_op jit(solution)/shard_map/add | solution.py:96
  (88 shorter events, 193.3 us)
Async XLA Ops:
  15.8 145.5 %all-to-all-start = ((f32[64,8,8,384]{3,2,0,1:T(8,128)}), f32[64,8,8,384]{3,2,0,1:T(8,128)}, u32[]{:S(2)}, u32[]{:S(2)}) async-start(f32[64,8,8,384]{3,2,0,1:T(8,128)} %bitcast.149), calls=%async_computation | async-start | bytes 12582912 | tf_op jit(solution)/shard_map/all_to_all | solution.py:127
  161.3 4.9 copy-start.16
  161.3 142.2 %all-to-all-start.2 = ((f32[64,8,8,384]{3,2,0,1:T(8,128)}), f32[64,8,8,384]{3,2,0,1:T(8,128)}, u32[]{:S(2)}, u32[]{:S(2)}) async-start(f32[64,8,8,384]{3,2,0,1:T(8,128)} %bitcast.145), calls=%async_computation.2 | async-start | bytes 12582912 | tf_op jit(solution)/shard_map/all_to_all | solution.py:127
  179.6 12.2 %copy-start.1 = (f32[3072,512]{1,0:T(8,128)S(1)}, f32[3072,512]{1,0:T(8,128)}, u32[]{:S(2)}) copy-start(f32[3072,512]{1,0:T(8,128)} %copy.33) | copy-start | bytes 18874372
  191.8 22.2 %slice-start = ((s8[6291456]{0:T(1024)(128)(4,1)}), s8[4194304]{0:T(1024)(128)(4,1)S(1)}, s32[]{:S(2)}) async-start(s8[6291456]{0:T(1024)(128)(4,1)} %bitcast.143), calls=%async_computation.6 | async-start | bytes 8388608
  203.4 10.6 slice-start.1
  208.0 3.8 copy-start.9
  208.0 4.5 copy-start.11
  212.5 136.5 %collective-permute-start = (f32[512,8,384]{0,2,1:T(8,128)}, f32[512,8,384]{0,2,1:T(8,128)}, u32[]{:S(2)}, u32[]{:S(2)}) collective-permute-start(f32[512,8,384]{0,2,1:T(8,128)} %pad_maximum_fusion.1), channel_id=1, source_target_pairs={{0,16},{8,24},{16,0},{24,8},{1,17},{9,25},{17,1},{25,9},{2,18},{10... | collective-permute-start | bytes 18874376 | tf_op jit(solution)/shard_map/ppermute | solution.py:16
  303.5 142.0 %all-to-all-start.4 = ((f32[64,8,8,384]{3,2,0,1:T(8,128)}), f32[64,8,8,384]{3,2,0,1:T(8,128)}, u32[]{:S(2)}, u32[]{:S(2)}) async-start(f32[64,8,8,384]{3,2,0,1:T(8,128)} %bitcast.140), calls=%async_computation.4 | async-start | bytes 12582912 | tf_op jit(solution)/shard_map/all_to_all | solution.py:127
  349.0 43.9 %collective-permute-start.1 = (f32[512,8,384]{0,2,1:T(8,128)}, f32[512,8,384]{0,2,1:T(8,128)}, u32[]{:S(2)}, u32[]{:S(2)}) collective-permute-start(f32[512,8,384]{0,2,1:T(8,128)} %collective-permute-done), channel_id=1, source_target_pairs={{0,8},{8,0},{16,24},{24,16},{1,9},{9,1},{17,25},{25,17},{2,10},{10... | collective-permute-start | bytes 18874376 | tf_op jit(solution)/shard_map/ppermute | solution.py:16
  362.9 12.2 %copy-start.2 = (f32[3072,512]{1,0:T(8,128)S(1)}, f32[3072,512]{1,0:T(8,128)}, u32[]{:S(2)}) copy-start(f32[3072,512]{1,0:T(8,128)} %copy.38) | copy-start | bytes 18874372
  386.6 4.8 copy-start.4
  386.6 6.3 copy-start.10
  386.6 6.3 copy-start.12
  391.4 138.2 %collective-permute-start.2 = (f32[512,8,384]{0,2,1:T(8,128)}, f32[512,8,384]{0,2,1:T(8,128)}, u32[]{:S(2)}, u32[]{:S(2)}) collective-permute-start(f32[512,8,384]{0,2,1:T(8,128)} %pad_maximum_fusion.3), channel_id=1, source_target_pairs={{0,16},{8,24},{16,0},{24,8},{1,17},{9,25},{17,1},{25,9},{2,18},{10... | collective-permute-start | bytes 18874376 | tf_op jit(solution)/shard_map/ppermute | solution.py:16
  445.4 174.2 %all-to-all-start.1 = ((f32[8,64,1,8,384]{4,3,1,2,0:T(8,128)}), f32[8,64,1,8,384]{4,3,1,2,0:T(8,128)}, u32[]{:S(2)}, u32[]{:S(2)}) async-start(f32[8,64,1,8,384]{4,3,1,2,0:T(8,128)} %bitcast.141), calls=%async_computation.1 | async-start | bytes 12582912 | tf_op jit(solution)/shard_map/all_to_all | solution.py:137
  529.6 48.6 %collective-permute-start.3 = (f32[512,8,384]{0,2,1:T(8,128)}, f32[512,8,384]{0,2,1:T(8,128)}, u32[]{:S(2)}, u32[]{:S(2)}) collective-permute-start(f32[512,8,384]{0,2,1:T(8,128)} %collective-permute-done.2), channel_id=1, source_target_pairs={{0,8},{8,0},{16,24},{24,16},{1,9},{9,1},{17,25},{25,17},{2,10},{10... | collective-permute-start | bytes 18874376 | tf_op jit(solution)/shard_map/ppermute | solution.py:16
  543.0 12.2 %copy-start.3 = (f32[3072,512]{1,0:T(8,128)S(1)}, f32[3072,512]{1,0:T(8,128)}, u32[]{:S(2)}) copy-start(f32[3072,512]{1,0:T(8,128)} %copy.43) | copy-start | bytes 18874372
  571.6 4.1 copy-start.6
  571.6 5.1 copy-start.8
  571.6 6.6 copy-start.5
  576.7 138.2 %collective-permute-start.4 = (f32[512,8,384]{0,2,1:T(8,128)}, f32[512,8,384]{0,2,1:T(8,128)}, u32[]{:S(2)}, u32[]{:S(2)}) collective-permute-start(f32[512,8,384]{0,2,1:T(8,128)} %pad_maximum_fusion.5), channel_id=1, source_target_pairs={{0,16},{8,24},{16,0},{24,8},{1,17},{9,25},{17,1},{25,9},{2,18},{10... | collective-permute-start | bytes 18874376 | tf_op jit(solution)/shard_map/ppermute | solution.py:16
  619.7 105.6 %copy-start.7 = (f32[512,8,192]{0,2,1:T(8,128)S(1)}, f32[512,8,192]{0,2,1:T(8,128)}, u32[]{:S(2)}) copy-start(f32[512,8,192]{0,2,1:T(8,128)} %copy-done.6) | copy-start | bytes 9437188
  619.7 148.1 %all-to-all-start.3 = ((f32[8,64,1,8,384]{4,3,1,2,0:T(8,128)}), f32[8,64,1,8,384]{4,3,1,2,0:T(8,128)}, u32[]{:S(2)}, u32[]{:S(2)}) async-start(f32[8,64,1,8,384]{4,3,1,2,0:T(8,128)} %bitcast.142), calls=%async_computation.3 | async-start | bytes 12582912 | tf_op jit(solution)/shard_map/all_to_all | solution.py:137
  715.0 10.4 collective-permute-start.5
  730.7 2.1 copy-start.14
  732.3 1.7 copy-start.15
  767.8 144.3 %all-to-all-start.5 = ((f32[8,64,1,8,384]{4,3,1,2,0:T(8,128)}), f32[8,64,1,8,384]{4,3,1,2,0:T(8,128)}, u32[]{:S(2)}, u32[]{:S(2)}) async-start(f32[8,64,1,8,384]{4,3,1,2,0:T(8,128)} %bitcast.146), calls=%async_computation.5 | async-start | bytes 12582912 | tf_op jit(solution)/shard_map/all_to_all | solution.py:137
  912.1 6.5 copy-start.13
  924.1 6.9 copy-start
